TPU v7x, 256 devices: a whole 4x4x8 slice. The times are simulated.
256 devices in a mesh: grp: 4 (over y), wide: 4 (over x_hi, core), blk: 16 (over z, x_lo).
Axes of the slice: x: 4 (x_hi: 2, x_lo: 2; x = x_hi * 2 + x_lo), y: 4, z: 8, core: 2. Of those that a mesh axis runs over, the one named last changes fastest.
Arguments:
- activations: bfloat16 [16384, 8192], P('blk', ('grp', 'wide')), may hold values from -6 to 6
- out_grads: bfloat16 [16384, 8192], P('blk', ('grp', 'wide')), may hold values from -6 to 6
- in_projection: bfloat16 [8192, 32], P(('grp', 'wide')), may hold values from -0.0625 to 0.0625
- out_projection: bfloat16 [8192, 64], P(('grp', 'wide')), may hold values from -0.0625 to 0.0625
- in_inverse: float32 [32, 32], replicated, may hold values from -1 to 1
- out_inverse: float32 [64, 64], replicated, may hold values from -0.75 to 0.75
- grad_store: bfloat16 [393216, 2048], P(('grp', 'wide', 'blk')), may hold values from -0.0234375 to 0.0234375
Outputs:
- influence: float32 [512, 393216], P(None, ('grp', 'wide', 'blk'))
All inputs are finite; a program needn't handle non-finite values.
Results may differ from a plain program's by a relative error of at most 0.0029.
Values may be sent and summed in bfloat16 or wider, within the bound.
A program may use at most 64 MiB of HBM per device.

v0:
```python
import jax
import jax.numpy as jnp
from jax import lax
from jax.sharding import PartitionSpec as P

SEQ = 32


highest = lax.Precision.HIGHEST


def over_pieces(shard, axis):
    return lax.all_gather(shard, axis).sum(0)


def joined_along(blocks, dim):
    blocks = jnp.moveaxis(blocks, 0, dim)
    lengths = blocks.shape
    return blocks.reshape(*lengths[:dim], lengths[dim] * lengths[dim + 1], *lengths[dim + 2 :])


def copy_for_each(shard, axis):
    copies = jnp.broadcast_to(shard, (lax.axis_size(axis), *shard.shape))
    return lax.all_to_all(copies, axis, split_axis=0, concat_axis=0, tiled=True)


def gather_directly(shard, axis, dim):
    return joined_along(copy_for_each(shard, axis), dim)


def partial_projection(activations, out_grads, in_projection, out_projection):
    contract = (((0,), (1,)), ((), ()))
    part_input = lax.dot_general(
        in_projection, activations, contract, preferred_element_type=jnp.float32
    )
    part_output = lax.dot_general(
        out_projection, out_grads, contract, preferred_element_type=jnp.float32
    )
    return jnp.concatenate([part_input, part_output], axis=0)


def build_queries(summed, in_inverse, out_inverse):
    width_in = in_inverse.shape[0]
    query_count = summed.shape[1] // SEQ
    low_input = summed[:width_in].reshape(width_in, query_count, SEQ)
    low_output = summed[width_in:].reshape(out_inverse.shape[0], query_count, SEQ)
    gradient = jnp.einsum("oqs,iqs->qoi", low_output, low_input, precision=highest)
    shaped = jnp.einsum("ao,qoi->qai", out_inverse, gradient, precision=highest)
    shaped = jnp.einsum("qai,ib->qab", shaped, in_inverse, precision=highest)
    return shaped.reshape(query_count, -1).astype(jnp.bfloat16)


def on_device(
    activations, out_grads, in_projection, out_projection, in_inverse, out_inverse, grad_store
):
    partial_sum = partial_projection(activations, out_grads, in_projection, out_projection)
    summed = over_pieces(partial_sum, ("grp", "wide"))
    queries = build_queries(summed, in_inverse, out_inverse)
    return lax.dot_general(
        gather_directly(queries, "blk", 0),
        grad_store,
        (((1,), (1,)), ((), ())),
        preferred_element_type=jnp.float32,
    )


def solution(mesh):
    return jax.shard_map(
        on_device,
        mesh=mesh,
        in_specs=(
            P("blk", ("grp", "wide")),
            P("blk", ("grp", "wide")),
            P(("grp", "wide"), None),
            P(("grp", "wide"), None),
            P(),
            P(),
            P(("grp", "wide", "blk"), None),
        ),
        out_specs=P(None, ("grp", "wide", "blk")),
        check_vma=False,
    )
```

profile of v0, /device:TPU:1, one launch (start us, length us, event | category | flops | bytes accessed | tf_op | source)
XLA Modules:
  0.0 161.6 jit_solution(1850931177654043275)
XLA Ops:
  6.5 0.0 copy-start
  6.5 0.0 all-gather.3.cloned.1.call-start
  6.5 1.7 %fusion.4 = f32[32,1024]{1,0:T(8,128)S(1)} fusion(bf16[512,32]{0,1:T(8,128)(2,1)} %param.9, bf16[1024,512]{1,0:T(8,128)(2,1)} %param.7), kind=kOutput, calls=%fused_computation.7 | convolution fusion | flops 33554432 | bytes 1212416 | tf_op jit(solution)/shard_map/dot_general | solution.py:33
  8.3 0.0 copy-done
  8.3 1.3 fusion.5
  9.6 0.8 pad_maximum_fusion
  10.3 0.0 all-gather.3.cloned.1.call-update
  10.4 73.1 %all-gather.3.cloned.1.call-done = f32[1536,1024]{1,0:T(8,128)} async-done(((f32[96,1024]{1,0:T(8,128)}), f32[1536,1024]{1,0:T(8,128)}) %all-gather.3.cloned.1.call-update) | async-done | bytes 6291472 | tf_op jit(solution)/shard_map/all_gather | solution.py:13
  83.4 3.4 %reduce_sum.9 = f32[96,1024]{1,0:T(8,128)S(1)} reduce(f32[16,96,1024]{2,1,0:T(8,128)} %bitcast.20, f32[]{:T(128)} %constant.0.clone.1), dimensions={0}, to_apply=%region_0.0 | reduce | flops 1474560 | bytes 6684676 | tf_op jit(solution)/shard_map/reduce_sum | solution.py:13
  86.8 0.0 copy-start.1
  86.8 0.0 copy-start.2
  86.9 0.2 copy.14
  87.1 0.2 reshape.12
  87.2 0.9 fusion
  88.1 0.0 copy-done.1
  88.1 0.6 convolution_bitcast_fusion
  88.7 0.0 copy-done.2
  88.7 0.6 convolution_convert_fusion
  89.3 0.3 copy.17
  89.6 0.5 convert_element_type.7
  90.2 0.2 broadcast_in_dim.3
  90.4 56.5 %all_to_all.5 = bf16[16,32,2048]{2,1,0:T(8,128)(2,1)S(1)} all-to-all(bf16[16,32,2048]{2,1,0:T(8,128)(2,1)S(1)} %broadcast_in_dim.3), channel_id=1, replica_groups=mesh['grp'=4,'wide'=4,'blk'=16] {'blk'}, dimensions={0} | all-to-all | bytes 4194304 | tf_op jit(solution)/shard_map/all_to_all | solution.py:24
  146.9 7.9 %fusion.6 = f32[512,1536]{1,0:T(8,128)} fusion(bf16[512,2048]{1,0:T(8,128)(2,1)S(1)} %bitcast.22, bf16[1536,2048]{1,0:T(8,128)(2,1)} %param.13), kind=kOutput, calls=%fused_computation.9 | convolution fusion | flops 3221225472 | bytes 11534336 | tf_op jit(solution)/shard_map/dot_general | solution.py:59
  (2 shorter events, 0.0 us)
Async XLA Ops:
  6.5 1.7 %copy-start = (bf16[1024,512]{1,0:T(8,128)(2,1)S(1)}, bf16[1024,512]{1,0:T(8,128)(2,1)}, u32[]{:S(2)}) copy-start(bf16[1024,512]{1,0:T(8,128)(2,1)} %param.8) | copy-start | bytes 3145732
  6.5 76.9 %all-gather.3.cloned.1.call-start = ((), (), s32[]{:S(2)}) async-start(), calls=%async_computation.1 | async-start | bytes 6684672 | tf_op jit(solution)/shard_map/all_gather | solution.py:13
  86.8 1.3 copy-start.1
  86.8 1.9 %copy-start.2 = (f32[32,32]{1,0:T(8,128)S(1)}, f32[32,32]{1,0:T(8,128)}, u32[]{:S(2)}) copy-start(f32[32,32]{1,0:T(8,128)} %param.11) | copy-start | bytes 12292
Sparse Core Ops, SparseCore 0:
  10.5 72.8 all-gather.2
where the time goes:
time: 162 us
  waiting for transfers between devices  73.1 us (45%)
  blocking collectives  56.5 us (35%)
  between operations  13.5 us (8%)
  matrix products  13 us (8%)
  other arithmetic  4.14 us (3%)
    all_gather x1, waiting for transfers between devices, over_pieces(): return lax.all_gather(shard, axis).sum(0)  73.1 us
    all_to_all x1, blocking collectives, copy_for_each(): return lax.all_to_all(copies, axis, split_axis=0, concat_axis=0, tiled=True)  56.5 us
    dot_general x1, matrix products, on_device(): lax.dot_general(gather_directly(queries, 'blk', 0), grad_store, (((1,), (...  7.9 us
    reduce_sum x1, other arithmetic, over_pieces(): return lax.all_gather(shard, axis).sum(0)  3.35 us
  transfers between devices with their start and end apart: 1, of which 1 were waited for; matrix products, arithmetic and copies ran while one was open for 0% of the time, Pallas kernels for 0%

commit v1 on v0

v1 whole, which is shorter than its diff:
```python
import functools

import jax
import jax.numpy as jnp
from jax import lax
from jax.experimental import pallas as pl
from jax.experimental.pallas import tpu as pltpu
from jax.sharding import PartitionSpec as P

SEQ = 32
MESH = pl.DeviceIdType.MESH
NT = (((1,), (1,)), ((), ()))
highest = lax.Precision.HIGHEST


def iota(shape, dim):
    return lax.broadcasted_iota(jnp.int32, shape, dim)


def dot32(a, b, dims=(((1,), (0,)), ((), ()))):
    return lax.dot_general(a, b, dims, precision=highest, preferred_element_type=jnp.float32)


def project(act_ref, grd_ref, win_ref, wout_ref, part):
    pairs = 2 * part.shape[0]
    k_in, depth = win_ref.shape
    k_out = wout_ref.shape[0]
    grads = grd_ref[...].reshape(pairs, 2, SEQ, depth)
    wout = wout_ref[...]
    blank = jnp.zeros((k_out, depth), wout.dtype)
    low = None
    for q in range(2):
        weight = jnp.concatenate([wout, blank] if q == 0 else [blank, wout], axis=0)
        rows = grads[:, q].reshape(pairs * SEQ, depth)
        term = lax.dot_general(rows, weight, NT, preferred_element_type=jnp.float32)
        low = term if low is None else low + term
    part[:, :, 0:SEQ, :] = low.reshape(pairs // 2, 2, SEQ, 128)
    acts = act_ref[...].reshape(pairs, 4, SEQ // 2, depth)
    win = win_ref[...]
    blank = jnp.zeros((k_in, depth), win.dtype)
    low = None
    for q in range(4):
        weight = jnp.concatenate([win if j == q else blank for j in range(4)], axis=0)
        rows = acts[:, q].reshape(pairs * SEQ // 2, depth)
        term = lax.dot_general(rows, weight, NT, preferred_element_type=jnp.float32)
        low = term if low is None else low + term
    part[:, :, SEQ:, :] = low.reshape(pairs // 2, 2, SEQ // 2, 128)


def factors(in_inverse, out_inverse):
    k_in, k_out = in_inverse.shape[0], out_inverse.shape[0]
    row, col = iota((128, k_out), 0), iota((128, k_out), 1)
    pick = jnp.where(col == 4 * ((row % 32) // 2) + row // 32, 1.0, 0.0).astype(jnp.float32)
    picked = dot32(pick, out_inverse)
    wide = jnp.concatenate([picked, picked], axis=1)
    row, col = iota((128, 128), 0), iota((128, 128), 1)
    left = jnp.where(col // k_out == row % 2, wide, 0.0)
    tall = jnp.concatenate([in_inverse] * 4, axis=0)
    right = jnp.concatenate([tall] * 4, axis=1)
    return left, right


def shape_queries(low, left, right):
    lo, li = low[:SEQ], low[SEQ:]
    first = dot32(lo[: SEQ // 2], li, (((0,), (0,)), ((), ())))
    second = dot32(lo[SEQ // 2 :], li, (((0,), (0,)), ((), ())))
    row, col = iota((128, 128), 0) // 64, iota((128, 128), 1) // 32
    gradient = jnp.where(col == 2 * row, first, jnp.where(col == 2 * row + 1, second, 0.0))
    both = dot32(left, dot32(gradient, right))
    lane = iota((32, 128), 1) // 32
    out = both[0:32]
    for k in range(1, 4):
        out = jnp.where(lane == k, both[32 * k : 32 * k + 32], out)
    return out


def comm_kernel(
    act_ref, grd_ref, win_ref, wout_ref, in_inv_ref, out_inv_ref,
    q_ref,
    part, from_core, half, from_group, mine,
    send_sem, recv_sem,
):
    y = lax.axis_index("grp")
    w = lax.axis_index("wide")
    b = lax.axis_index("blk")
    ny, nz = 4, 8
    xh, c = w // 2, w % 2
    z, xl = b // 2, b % 2
    x = 2 * xh + xl
    oc = 1 - c

    def device(y_, x_, z_, c_):
        return (y_, 2 * (x_ // 2) + c_, 2 * z_ + x_ % 2)

    group = [(dy, dx) for dy in range(ny) for dx in (0, 2) if (dy, dx) != (0, 0)]
    partner = device(y, x, z, oc)
    to_group = [device((y + dy) % ny, (x + dx) % 4, z, c) for dy, dx in group]
    to_z = [device(y, x, (z + d) % nz, c) for d in range(1, nz)]
    to_x = [device(y, (x + d) % 4, z, c) for d in range(1, 4)]
    to_y = [device((y + d) % ny, x, z, c) for d in range(1, ny)]

    barrier = pltpu.get_barrier_semaphore()
    greeted = [partner] + to_group + to_z + [to_x[0], to_x[2]]
    for peer in greeted:
        pl.semaphore_signal(barrier, inc=1, device_id=peer, device_id_type=MESH)

    project(act_ref, grd_ref, win_ref, wout_ref, part)

    pl.semaphore_wait(barrier, len(greeted))

    used = []

    def copy(src, dst, peer):
        n = len(used)
        used.append(
            pltpu.make_async_remote_copy(
                src_ref=src, dst_ref=dst, send_sem=send_sem.at[n], recv_sem=recv_sem.at[n],
                device_id=peer, device_id_type=MESH,
            )
        )
        return used[-1]

    core = copy(part.at[:, oc], from_core, partner)
    core.start()
    left, right = factors(in_inv_ref[...], out_inv_ref[...])
    core.wait_recv()
    half[...] = part[:, c] + from_core[...]

    sums = []
    for n, (dy, dx) in enumerate(group):
        target = ((y + dy) % ny) * 2 + ((x + dx) % 4) // 2
        sums.append(copy(half.at[target], from_group.at[n], to_group[n]))
        sums[-1].start()
    low = half[y * 2 + xh]
    for n, one in enumerate(sums):
        one.wait_recv()
        low = low + from_group[n]

    rows = shape_queries(low, left, right).astype(jnp.bfloat16)
    for j in range(16):
        mine[j] = rows[2 * j : 2 * j + 2]

    lo_slab, other = 8 * c, 8 * oc
    own = pl.ds(lo_slab, 8)
    swap = copy(mine.at[pl.ds(other, 8)], q_ref.at[pl.ds(other, 8), z, xl, y, xh, c], partner)
    swap.start()
    q_ref[own, z, xl, y, xh, c] = mine[own]
    swap.wait_recv()

    column = q_ref.at[own, z, xl, y, xh]
    stage = [copy(column, column, peer) for peer in to_z]
    for one in stage:
        one.start()
    for one in stage:
        one.wait_recv()

    a, bb = pl.ds(lo_slab, 4), pl.ds(lo_slab + 4, 4)
    a1 = [copy(q_ref.at[a, :, xl, y, xh], q_ref.at[a, :, xl, y, xh], peer) for peer in to_x]
    b1 = [copy(q_ref.at[bb, :, xl, y, xh], q_ref.at[bb, :, xl, y, xh], peer) for peer in to_y]
    for one in a1 + b1:
        one.start()
    for one in a1:
        one.wait_recv()
    a2 = [copy(q_ref.at[a, :, :, y], q_ref.at[a, :, :, y], peer) for peer in to_y]
    for one in a2:
        one.start()
    for one in b1:
        one.wait_recv()
    b2 = [copy(q_ref.at[bb, :, xl, :, xh], q_ref.at[bb, :, xl, :, xh], peer) for peer in to_x]
    for one in b2:
        one.start()
    last = []
    for stage, span in ((a2, a), (b2, bb)):
        for one in stage:
            one.wait_recv()
        last.append(copy(q_ref.at[span], q_ref.at[span], partner))
        last[-1].start()
    for one in last:
        one.wait_recv()
    for one in used:
        one.wait_send()


COPIES = 1 + 7 + 1 + 7 + 3 * 4 + 2


def gather_queries(activations, out_grads, in_projection, out_projection, in_inverse, out_inverse):
    pairs = activations.shape[0] // (2 * SEQ)
    vmem = pl.BlockSpec(memory_space=pltpu.VMEM)
    kern = pl.pallas_call(
        lambda a, g, wi, wo, ii, oi, q, part, fc, *rest: comm_kernel(
            a, g, wi, wo, ii, oi, q, part, fc, *rest
        ),
        out_shape=jax.ShapeDtypeStruct((16, 8, 2, 4, 2, 2, 2, 128), jnp.bfloat16),
        in_specs=[vmem] * 6,
        out_specs=vmem,
        scratch_shapes=[
            pltpu.VMEM((pairs // 2, 2, 48, 128), jnp.float32),
            pltpu.VMEM((pairs // 2, 48, 128), jnp.float32),
            pltpu.VMEM((pairs // 2, 48, 128), jnp.float32),
            pltpu.VMEM((7, 48, 128), jnp.float32),
            pltpu.VMEM((16, 2, 128), jnp.bfloat16),
            pltpu.SemaphoreType.DMA((COPIES,)),
            pltpu.SemaphoreType.DMA((COPIES,)),
        ],
        compiler_params=pltpu.CompilerParams(
            collective_id=0, has_side_effects=True, vmem_limit_bytes=32 * 1024 * 1024
        ),
    )
    return kern(activations, out_grads, in_projection.T, out_projection.T, in_inverse, out_inverse)


def product_kernel(q_ref, s_ref, o_ref):
    queries = jnp.concatenate([q_ref[j] for j in range(16)], axis=1)
    o_ref[...] = lax.dot_general(queries, s_ref[...], NT, preferred_element_type=jnp.float32)


def product(queries, store):
    rows, depth = store.shape
    block = 256
    return pl.pallas_call(
        product_kernel,
        out_shape=jax.ShapeDtypeStruct((512, rows), jnp.float32),
        grid=(rows // block,),
        in_specs=[
            pl.BlockSpec((16, 512, 128), lambda i: (0, 0, 0)),
            pl.BlockSpec((block, depth), lambda i: (i, 0)),
        ],
        out_specs=pl.BlockSpec((512, block), lambda i: (0, i)),
    )(queries, store)


def on_device(
    activations, out_grads, in_projection, out_projection, in_inverse, out_inverse, grad_store
):
    gathered = gather_queries(
        activations, out_grads, in_projection, out_projection, in_inverse, out_inverse
    )
    return product(gathered.reshape(16, 512, 128), grad_store)


def solution(mesh):
    return jax.shard_map(
        on_device,
        mesh=mesh,
        in_specs=(
            P("blk", ("grp", "wide")),
            P("blk", ("grp", "wide")),
            P(("grp", "wide"), None),
            P(("grp", "wide"), None),
            P(),
            P(),
            P(("grp", "wide", "blk"), None),
        ),
        out_specs=P(None, ("grp", "wide", "blk")),
        check_vma=False,
    )
```

time: 162 us -> 54.7 us (0.34)
  waiting for transfers between devices: 73.1 us -> 0 us
  blocking collectives: 56.5 us -> 0 us
  Pallas kernels: 0 us -> 47.3 us
  between operations: 13.5 us -> 0.02 us
  matrix products: 13 us -> 0 us
  local copies, waits for them, and re-layouts: 1.48 us -> 6.87 us
  other arithmetic: 4.14 us -> 0 us
    all_gather x1 -> x0, waiting for transfers between devices: 73.1 us -> none  [over_pieces(): return lax.all_gather(shard, axis).sum(0)]
    all_to_all x1 -> x0, blocking collectives: 56.5 us -> none  [copy_for_each(): return lax.all_to_all(copies, axis, split_axis=0, concat_axis=0, tiled=True)]
    pallas_call x0 -> x2, Pallas kernels: none -> 47.3 us  [the longest x1 38.6 us: gather_queries(): kern(activations, out_grads, in_projection.T, out_projection.T, in_invers...]
    dot_general x6 -> x0, matrix products: 13 us -> none  [the longest x1 7.9 us: on_device(): lax.dot_general(gather_directly(queries, 'blk', 0), grad_store, (((1,), (...]
    unnamed x6 -> x14, local copies, waits for them, and re-layouts: 0.03 us -> 6.87 us
    reduce_sum x1 -> x0, other arithmetic: 3.35 us -> none  [over_pieces(): return lax.all_gather(shard, axis).sum(0)]
  transfers between devices with their start and end apart: 1 -> 0, of which waited for: 1 -> 0; matrix products, arithmetic and copies ran while one was open for 0% -> 0% of each run, Pallas kernels for 0% -> 0%
where the time goes in v1:
time: 54.7 us; the launch traced here: 54.2 us
  Pallas kernels  47.3 us (86%)
  local copies, waits for them, and re-layouts  6.87 us (13%)
    pallas_call x1, Pallas kernels, gather_queries(): kern(activations, out_grads, in_projection.T, out_projection.T, in_invers...  38.6 us
    pallas_call x1, Pallas kernels, product(): pl.pallas_call(product_kernel, out_shape=jax.ShapeDtypeStruct((512, rows)...  8.71 us
    unnamed x14, local copies, waits for them, and re-layouts  6.87 us

profile of v1, /device:TPU:1, one launch (start us, length us, event | category | flops | bytes accessed | tf_op | source)
XLA Modules:
  0.0 54.2 jit_solution(14918787623396859232)
XLA Ops:
  0.0 0.0 copy-start.1
  0.0 1.2 %copy-done.1 = bf16[1024,512]{1,0:T(8,128)(2,1)S(1)} copy-done((bf16[1024,512]{1,0:T(8,128)(2,1)S(1)}, bf16[1024,512]{1,0:T(8,128)(2,1)}, u32[]{:S(2)}) %copy-start.1) | copy-done | bytes 1048600
  1.2 0.0 copy-start.2
  1.2 1.2 %copy-done.2 = bf16[1024,512]{1,0:T(8,128)(2,1)S(1)} copy-done((bf16[1024,512]{1,0:T(8,128)(2,1)S(1)}, bf16[1024,512]{1,0:T(8,128)(2,1)}, u32[]{:S(2)}) %copy-start.2) | copy-done | bytes 1048600
  2.5 0.0 copy-start.3
  2.5 0.8 %copy-done.3 = bf16[512,64]{0,1:T(8,128)(2,1)S(1)} copy-done((bf16[512,64]{0,1:T(8,128)(2,1)S(1)}, bf16[512,64]{0,1:T(8,128)(2,1)}, u32[]{:S(2)}) %copy-start.3) | copy-done | bytes 65560
  3.3 0.0 copy-start.4
  3.3 0.8 %copy-done.4 = bf16[512,32]{0,1:T(8,128)(2,1)S(1)} copy-done((bf16[512,32]{0,1:T(8,128)(2,1)S(1)}, bf16[512,32]{0,1:T(8,128)(2,1)}, u32[]{:S(2)}) %copy-start.4) | copy-done | bytes 32792
  4.0 0.0 copy-start.5
  4.1 0.8 %copy-done.5 = f32[64,64]{1,0:T(8,128)S(1)} copy-done((f32[64,64]{1,0:T(8,128)S(1)}, f32[64,64]{1,0:T(8,128)}, u32[]{:S(2)}) %copy-start.5) | copy-done | bytes 16408
  4.8 0.0 copy-start.6
  4.8 0.7 %copy-done.6 = f32[32,32]{1,0:T(8,128)S(1)} copy-done((f32[32,32]{1,0:T(8,128)S(1)}, f32[32,32]{1,0:T(8,128)}, u32[]{:S(2)}) %copy-start.6) | copy-done | bytes 4120
  5.5 38.6 %shard_map.73 = bf16[16,8,2,4,2,2,2,128]{7,6,5,4,3,2,1,0:T(2,128)(2,1)S(1)} custom-call(bf16[1024,512]{1,0:T(8,128)(2,1)S(1)} %copy-done.1, bf16[1024,512]{1,0:T(8,128)(2,1)S(1)} %copy-done.2, bf16[32,512]{1,0:T(8,128)(2,1)S(1)} %bitcast.5, bf16[64,512]{1,0:T(8,128)(2,1)S(1)} %bitcast.4, f32[32,32]{1,0:T(8,128)S(1)} %copy-done.6, f32[64,64]{1,0:T(8,128)S(1)} %copy-done.5), custom_call_target="tpu_custom_call" | custom-call | tf_op jit(solution)/shard_map/pallas_call | solution.py:210
  44.1 0.0 copy-start
  44.1 1.3 %copy-done = bf16[16,8,2,4,2,2,2,128]{7,6,5,4,3,2,1,0:T(2,128)(2,1)} copy-done((bf16[16,8,2,4,2,2,2,128]{7,6,5,4,3,2,1,0:T(2,128)(2,1)}, bf16[16,8,2,4,2,2,2,128]{7,6,5,4,3,2,1,0:T(2,128)(2,1)S(1)}, u32[]{:S(2)}) %copy-start) | copy-done | bytes 2097176
  45.4 8.7 %shard_map.74 = f32[512,1536]{1,0:T(8,128)} custom-call(bf16[16,512,128]{2,1,0:T(8,128)(2,1)} %bitcast.3, bf16[1536,2048]{1,0:T(8,128)(2,1)} %s_ref.1), custom_call_target="tpu_custom_call" | custom-call | tf_op jit(solution)/shard_map/pallas_call | solution.py:221
Async XLA Ops:
  0.0 1.2 %copy-start.1 = (bf16[1024,512]{1,0:T(8,128)(2,1)S(1)}, bf16[1024,512]{1,0:T(8,128)(2,1)}, u32[]{:S(2)}) copy-start(bf16[1024,512]{1,0:T(8,128)(2,1)} %a.1) | copy-start | bytes 3145732
  1.2 1.2 %copy-start.2 = (bf16[1024,512]{1,0:T(8,128)(2,1)S(1)}, bf16[1024,512]{1,0:T(8,128)(2,1)}, u32[]{:S(2)}) copy-start(bf16[1024,512]{1,0:T(8,128)(2,1)} %g.1) | copy-start | bytes 3145732
  2.5 0.8 %copy-start.3 = (bf16[512,64]{0,1:T(8,128)(2,1)S(1)}, bf16[512,64]{0,1:T(8,128)(2,1)}, u32[]{:S(2)}) copy-start(bf16[512,64]{0,1:T(8,128)(2,1)} %param.10) | copy-start | bytes 196612
  3.3 0.8 %copy-start.4 = (bf16[512,32]{0,1:T(8,128)(2,1)S(1)}, bf16[512,32]{0,1:T(8,128)(2,1)}, u32[]{:S(2)}) copy-start(bf16[512,32]{0,1:T(8,128)(2,1)} %param.9) | copy-start | bytes 98308
  4.0 0.8 %copy-start.5 = (f32[64,64]{1,0:T(8,128)S(1)}, f32[64,64]{1,0:T(8,128)}, u32[]{:S(2)}) copy-start(f32[64,64]{1,0:T(8,128)} %oi.1) | copy-start | bytes 49156
  4.8 0.7 %copy-start.6 = (f32[32,32]{1,0:T(8,128)S(1)}, f32[32,32]{1,0:T(8,128)}, u32[]{:S(2)}) copy-start(f32[32,32]{1,0:T(8,128)} %ii.1) | copy-start | bytes 12292
  44.1 1.4 %copy-start = (bf16[16,8,2,4,2,2,2,128]{7,6,5,4,3,2,1,0:T(2,128)(2,1)}, bf16[16,8,2,4,2,2,2,128]{7,6,5,4,3,2,1,0:T(2,128)(2,1)S(1)}, u32[]{:S(2)}) copy-start(bf16[16,8,2,4,2,2,2,128]{7,6,5,4,3,2,1,0:T(2,128)(2,1)S(1)} %shard_map.73) | copy-start | bytes 6291460

commit v2 on v1

--- a/solution.py
+++ b/solution.py
@@ -21,10 +21,11 @@
     return lax.dot_general(a, b, dims, precision=highest, preferred_element_type=jnp.float32)
 
 
-def project(act_ref, grd_ref, win_ref, wout_ref, part):
+def project(act_ref, grd_ref, win_ref, wout_ref, part, ready_grad, ready_act):
     pairs = 2 * part.shape[0]
     k_in, depth = win_ref.shape
     k_out = wout_ref.shape[0]
+    ready_grad()
     grads = grd_ref[...].reshape(pairs, 2, SEQ, depth)
     wout = wout_ref[...]
     blank = jnp.zeros((k_out, depth), wout.dtype)
@@ -35,6 +36,7 @@
         term = lax.dot_general(rows, weight, NT, preferred_element_type=jnp.float32)
         low = term if low is None else low + term
     part[:, :, 0:SEQ, :] = low.reshape(pairs // 2, 2, SEQ, 128)
+    ready_act()
     acts = act_ref[...].reshape(pairs, 4, SEQ // 2, depth)
     win = win_ref[...]
     blank = jnp.zeros((k_in, depth), win.dtype)
@@ -75,11 +77,22 @@
 
 
 def comm_kernel(
+    act_hbm, grd_hbm, win_hbm, wout_hbm, in_inv_hbm, out_inv_hbm,
+    q_ref,
     act_ref, grd_ref, win_ref, wout_ref, in_inv_ref, out_inv_ref,
-    q_ref,
     part, from_core, half, from_group, mine,
-    send_sem, recv_sem,
+    load_sem, send_sem, recv_sem,
 ):
+    loads = [
+        pltpu.make_async_copy(src, dst, load_sem.at[n])
+        for n, (src, dst) in enumerate((
+            (wout_hbm, wout_ref), (grd_hbm, grd_ref), (win_hbm, win_ref), (act_hbm, act_ref),
+            (in_inv_hbm, in_inv_ref), (out_inv_hbm, out_inv_ref),
+        ))
+    ]
+    for one in loads:
+        one.start()
+
     y = lax.axis_index("grp")
     w = lax.axis_index("wide")
     b = lax.axis_index("blk")
@@ -104,7 +117,14 @@
     for peer in greeted:
         pl.semaphore_signal(barrier, inc=1, device_id=peer, device_id_type=MESH)
 
-    project(act_ref, grd_ref, win_ref, wout_ref, part)
+    def arrived(first, stop):
+        for one in loads[first:stop]:
+            one.wait()
+
+    project(
+        act_ref, grd_ref, win_ref, wout_ref, part, lambda: arrived(0, 2), lambda: arrived(2, 4)
+    )
+    arrived(4, 6)
 
     pl.semaphore_wait(barrier, len(greeted))
 
@@ -186,28 +206,30 @@
 
 def gather_queries(activations, out_grads, in_projection, out_projection, in_inverse, out_inverse):
     pairs = activations.shape[0] // (2 * SEQ)
-    vmem = pl.BlockSpec(memory_space=pltpu.VMEM)
+    operands = (
+        activations, out_grads, in_projection.T, out_projection.T, in_inverse, out_inverse
+    )
     kern = pl.pallas_call(
-        lambda a, g, wi, wo, ii, oi, q, part, fc, *rest: comm_kernel(
-            a, g, wi, wo, ii, oi, q, part, fc, *rest
-        ),
+        comm_kernel,
         out_shape=jax.ShapeDtypeStruct((16, 8, 2, 4, 2, 2, 2, 128), jnp.bfloat16),
-        in_specs=[vmem] * 6,
-        out_specs=vmem,
+        in_specs=[pl.BlockSpec(memory_space=pl.ANY)] * len(operands),
+        out_specs=pl.BlockSpec(memory_space=pltpu.VMEM),
         scratch_shapes=[
+            *[pltpu.VMEM(one.shape, one.dtype) for one in operands],
             pltpu.VMEM((pairs // 2, 2, 48, 128), jnp.float32),
             pltpu.VMEM((pairs // 2, 48, 128), jnp.float32),
             pltpu.VMEM((pairs // 2, 48, 128), jnp.float32),
             pltpu.VMEM((7, 48, 128), jnp.float32),
             pltpu.VMEM((16, 2, 128), jnp.bfloat16),
+            pltpu.SemaphoreType.DMA((len(operands),)),
             pltpu.SemaphoreType.DMA((COPIES,)),
             pltpu.SemaphoreType.DMA((COPIES,)),
         ],
         compiler_params=pltpu.CompilerParams(
-            collective_id=0, has_side_effects=True, vmem_limit_bytes=32 * 1024 * 1024
+            collective_id=0, has_side_effects=True, vmem_limit_bytes=60 * 1024 * 1024
         ),
     )
-    return kern(activations, out_grads, in_projection.T, out_projection.T, in_inverse, out_inverse)
+    return kern(*operands)
 
 
 def product_kernel(q_ref, s_ref, o_ref):

time: 54.7 us -> 49 us (0.90)
  local copies, waits for them, and re-layouts: 6.87 us -> 0 us
  Pallas kernels: 47.3 us -> 48.8 us
    unnamed x14 -> x0, local copies, waits for them, and re-layouts: 6.87 us -> none
    pallas_call x1, Pallas kernels: 38.6 us -> 40 us  [gather_queries(): return kern(*operands)]
where the time goes in v2:
time: 49 us; the launch traced here: 48.8 us
  Pallas kernels  48.8 us (100%)
    pallas_call x1, Pallas kernels, gather_queries(): return kern(*operands)  40 us
    pallas_call x1, Pallas kernels, product(): pl.pallas_call(product_kernel, out_shape=jax.ShapeDtypeStruct((512, rows)...  8.73 us

profile of v2, /device:TPU:1, one launch (start us, length us, event | category | flops | bytes accessed | tf_op | source)
XLA Modules:
  0.0 48.8 jit_solution(9926129969914524504)
XLA Ops:
  0.0 40.0 %shard_map.73 = bf16[16,8,2,4,2,2,2,128]{7,6,5,4,3,2,1,0:T(2,128)(2,1)} custom-call(bf16[1024,512]{1,0:T(8,128)(2,1)} %act_hbm.1, bf16[1024,512]{1,0:T(8,128)(2,1)} %grd_hbm.1, bf16[32,512]{1,0:T(8,128)(2,1)} %bitcast.5, bf16[64,512]{1,0:T(8,128)(2,1)} %bitcast.4, f32[32,32]{1,0:T(8,128)} %in_inv_hbm.1, f32[64,64]{1,0:T(8,128)} %out_inv_hbm.1), custom_call_target="tpu_custom_call" | custom-call | tf_op jit(solution)/shard_map/pallas_call | solution.py:232
  40.0 8.7 %shard_map.74 = f32[512,1536]{1,0:T(8,128)} custom-call(bf16[16,512,128]{2,1,0:T(8,128)(2,1)} %bitcast.3, bf16[1536,2048]{1,0:T(8,128)(2,1)} %s_ref.1), custom_call_target="tpu_custom_call" | custom-call | tf_op jit(solution)/shard_map/pallas_call | solution.py:243

commit v3 on v2

--- a/solution.py
+++ b/solution.py
@@ -76,11 +76,11 @@
     return out
 
 
-def comm_kernel(
-    act_hbm, grd_hbm, win_hbm, wout_hbm, in_inv_hbm, out_inv_hbm,
-    q_ref,
-    act_ref, grd_ref, win_ref, wout_ref, in_inv_ref, out_inv_ref,
-    part, from_core, half, from_group, mine,
+def influence_kernel(
+    act_hbm, grd_hbm, win_hbm, wout_hbm, in_inv_hbm, out_inv_hbm, store_hbm,
+    out_ref,
+    act_ref, grd_ref, win_ref, wout_ref, in_inv_ref, out_inv_ref, store,
+    part, from_core, half, from_group, mine, queries,
     load_sem, send_sem, recv_sem,
 ):
     loads = [
@@ -125,6 +125,8 @@
         act_ref, grd_ref, win_ref, wout_ref, part, lambda: arrived(0, 2), lambda: arrived(2, 4)
     )
     arrived(4, 6)
+    load_store = pltpu.make_async_copy(store_hbm, store, load_sem.at[len(loads)])
+    load_store.start()
 
     pl.semaphore_wait(barrier, len(greeted))
 
@@ -160,58 +162,104 @@
     for j in range(16):
         mine[j] = rows[2 * j : 2 * j + 2]
 
-    lo_slab, other = 8 * c, 8 * oc
-    own = pl.ds(lo_slab, 8)
-    swap = copy(mine.at[pl.ds(other, 8)], q_ref.at[pl.ds(other, 8), z, xl, y, xh, c], partner)
+    base, other = 8 * c, 8 * oc
+    own = pl.ds(base, 8)
+    swap = copy(mine.at[pl.ds(other, 8)], queries.at[pl.ds(other, 8), z, xl, y, xh, c], partner)
     swap.start()
-    q_ref[own, z, xl, y, xh, c] = mine[own]
+    queries[own, z, xl, y, xh, c] = mine[own]
     swap.wait_recv()
 
-    column = q_ref.at[own, z, xl, y, xh]
-    stage = [copy(column, column, peer) for peer in to_z]
-    for one in stage:
-        one.start()
-    for one in stage:
-        one.wait_recv()
-
-    a, bb = pl.ds(lo_slab, 4), pl.ds(lo_slab + 4, 4)
-    a1 = [copy(q_ref.at[a, :, xl, y, xh], q_ref.at[a, :, xl, y, xh], peer) for peer in to_x]
-    b1 = [copy(q_ref.at[bb, :, xl, y, xh], q_ref.at[bb, :, xl, y, xh], peer) for peer in to_y]
-    for one in a1 + b1:
-        one.start()
-    for one in a1:
-        one.wait_recv()
-    a2 = [copy(q_ref.at[a, :, :, y], q_ref.at[a, :, :, y], peer) for peer in to_y]
-    for one in a2:
-        one.start()
-    for one in b1:
-        one.wait_recv()
-    b2 = [copy(q_ref.at[bb, :, xl, :, xh], q_ref.at[bb, :, xl, :, xh], peer) for peer in to_x]
-    for one in b2:
-        one.start()
-    last = []
-    for stage, span in ((a2, a), (b2, bb)):
-        for one in stage:
+    def send(view, peers):
+        sent = [copy(view, view, peer) for peer in peers]
+        for one in sent:
+            one.start()
+        return sent
+
+    def arrive(sent):
+        for one in sent:
             one.wait_recv()
-        last.append(copy(q_ref.at[span], q_ref.at[span], partner))
-        last[-1].start()
-    for one in last:
-        one.wait_recv()
+
+    def line(s, x_, y_):
+        return (
+            queries.at[base + 2 * s, :, x_ % 2, y, x_ // 2],
+            queries.at[base + 2 * s + 1, :, xl, y_, xh],
+        )
+
+    def plane(s, x_, y_):
+        return (
+            queries.at[base + 2 * s, :, :, y_],
+            queries.at[base + 2 * s + 1, :, x_ % 2, :, x_ // 2],
+        )
+
+    CHUNKS = 4
+    columns = [send(queries.at[pl.ds(base, 2), z, xl, y, xh], to_z)]
+    columns.append(send(queries.at[pl.ds(base + 2, 6), z, xl, y, xh], to_z))
+    lines = []
+    for s in range(CHUNKS):
+        if s < 2:
+            arrive(columns[s])
+        along_x, along_y = line(s, x, y)
+        lines.append(send(along_x, to_x) + send(along_y, to_y))
+    planes = []
+    for s in range(CHUNKS):
+        arrive(lines[s])
+        along_y, along_x = plane(s, x, y)
+        planes.append(
+            send(along_y, [to_y[0], to_y[2]]) + send(along_x, [to_x[0], to_x[2]])
+        )
+    passed = []
+    for s in range(CHUNKS):
+        arrive(planes[s])
+        step, ahead = (3, 0) if s % 2 == 0 else (1, 2)
+        along_y, along_x = plane(s, (x + step) % 4, (y + step) % 4)
+        passed.append(send(along_y, [to_y[ahead]]) + send(along_x, [to_x[ahead]]))
+
+    view = queries.reshape(16, 512, 128)
+
+    def add_product(slab, first):
+        rows = jnp.concatenate([view[slab], view[slab + 1]], axis=1)
+        column = pl.ds(pl.multiple_of(slab * 128, 256), 256)
+
+        def tile(n, _):
+            part_rows = pl.ds(pl.multiple_of(n * 256, 256), 256)
+            term = lax.dot_general(
+                rows, store[part_rows, column], NT, preferred_element_type=jnp.float32
+            )
+            if first:
+                out_ref[:, part_rows] = term
+            else:
+                out_ref[:, part_rows] += term
+            return 0
+
+        lax.fori_loop(0, store.shape[0] // 256, tile, 0)
+
+    load_store.wait()
+    swaps = []
+    for s in range(CHUNKS):
+        arrive(passed[s])
+        swaps.append(send(queries.at[pl.ds(base + 2 * s, 2)], [partner]))
+        add_product(base + 2 * s, s == 0)
+    for s in range(CHUNKS):
+        arrive(swaps[s])
+        add_product(other + 2 * s, False)
     for one in used:
         one.wait_send()
 
 
-COPIES = 1 + 7 + 1 + 7 + 3 * 4 + 2
-
-
-def gather_queries(activations, out_grads, in_projection, out_projection, in_inverse, out_inverse):
+COPIES = 1 + 7 + 1 + 2 * 7 + 4 * (6 + 4 + 2 + 1)
+
+
+def on_device(
+    activations, out_grads, in_projection, out_projection, in_inverse, out_inverse, grad_store
+):
     pairs = activations.shape[0] // (2 * SEQ)
     operands = (
-        activations, out_grads, in_projection.T, out_projection.T, in_inverse, out_inverse
+        activations, out_grads, in_projection.T, out_projection.T, in_inverse, out_inverse,
+        grad_store,
     )
     kern = pl.pallas_call(
-        comm_kernel,
-        out_shape=jax.ShapeDtypeStruct((16, 8, 2, 4, 2, 2, 2, 128), jnp.bfloat16),
+        influence_kernel,
+        out_shape=jax.ShapeDtypeStruct((512, grad_store.shape[0]), jnp.float32),
         in_specs=[pl.BlockSpec(memory_space=pl.ANY)] * len(operands),
         out_specs=pl.BlockSpec(memory_space=pltpu.VMEM),
         scratch_shapes=[
@@ -221,6 +269,7 @@
             pltpu.VMEM((pairs // 2, 48, 128), jnp.float32),
             pltpu.VMEM((7, 48, 128), jnp.float32),
             pltpu.VMEM((16, 2, 128), jnp.bfloat16),
+            pltpu.VMEM((16, 8, 2, 4, 2, 2, 2, 128), jnp.bfloat16),
             pltpu.SemaphoreType.DMA((len(operands),)),
             pltpu.SemaphoreType.DMA((COPIES,)),
             pltpu.SemaphoreType.DMA((COPIES,)),
@@ -230,35 +279,6 @@
         ),
     )
     return kern(*operands)
-
-
-def product_kernel(q_ref, s_ref, o_ref):
-    queries = jnp.concatenate([q_ref[j] for j in range(16)], axis=1)
-    o_ref[...] = lax.dot_general(queries, s_ref[...], NT, preferred_element_type=jnp.float32)
-
-
-def product(queries, store):
-    rows, depth = store.shape
-    block = 256
-    return pl.pallas_call(
-        product_kernel,
-        out_shape=jax.ShapeDtypeStruct((512, rows), jnp.float32),
-        grid=(rows // block,),
-        in_specs=[
-            pl.BlockSpec((16, 512, 128), lambda i: (0, 0, 0)),
-            pl.BlockSpec((block, depth), lambda i: (i, 0)),
-        ],
-        out_specs=pl.BlockSpec((512, block), lambda i: (0, i)),
-    )(queries, store)
-
-
-def on_device(
-    activations, out_grads, in_projection, out_projection, in_inverse, out_inverse, grad_store
-):
-    gathered = gather_queries(
-        activations, out_grads, in_projection, out_projection, in_inverse, out_inverse
-    )
-    return product(gathered.reshape(16, 512, 128), grad_store)
 
 
 def solution(mesh):

time: 49 us -> 53.5 us (1.092)
  the two profiles are of different devices: /device:TPU:1 before, /device:TPU:2 now
where the time goes in v3:
time: 53.5 us; the launch traced here: 53.4 us
  Pallas kernels  49.6 us (93%)
  local copies, waits for them, and re-layouts  3.76 us (7%)
    pallas_call x1, Pallas kernels, on_device(): return kern(*operands)  49.6 us
    unnamed x1, local copies, waits for them, and re-layouts  3.76 us

profile of v3, /device:TPU:2, one launch (start us, length us, event | category | flops | bytes accessed | tf_op | source)
XLA Modules:
  0.0 53.4 jit_solution(17336335620687860154)
XLA Ops:
  0.0 49.6 %shard_map.73 = f32[512,1536]{1,0:T(8,128)} custom-call(bf16[1024,512]{1,0:T(8,128)(2,1)} %act_hbm.1, bf16[1024,512]{1,0:T(8,128)(2,1)} %grd_hbm.1, bf16[32,512]{1,0:T(8,128)(2,1)} %bitcast.3, bf16[64,512]{1,0:T(8,128)(2,1)} %bitcast.2, f32[32,32]{1,0:T(8,128)} %in_inv_hbm.1, f32[64,64]{1,0:T(8,128)} %out_inv_hbm.1, bf16[1536,2048]{1,0:T(8,128)(2,1)} %store_hbm.1), custom_call_target="tpu_custom_call" | custom-call | tf_op jit(solution)/shard_map/pallas_call | solution.py:281
  49.6 3.8 %copy.9 = f32[512,1536]{1,0:T(8,128)} copy(f32[512,1536]{1,0:T(8,128)} %shard_map.73) | data formatting | bytes 6291456

commit v4 on v3

--- a/solution.py
+++ b/solution.py
@@ -8,6 +8,7 @@
 from jax.sharding import PartitionSpec as P
 
 SEQ = 32
+SPAN = 8
 MESH = pl.DeviceIdType.MESH
 NT = (((1,), (1,)), ((), ()))
 highest = lax.Precision.HIGHEST
@@ -205,20 +206,13 @@
         arrive(lines[s])
         along_y, along_x = plane(s, x, y)
         planes.append(
-            send(along_y, [to_y[0], to_y[2]]) + send(along_x, [to_x[0], to_x[2]])
-        )
-    passed = []
-    for s in range(CHUNKS):
-        arrive(planes[s])
-        step, ahead = (3, 0) if s % 2 == 0 else (1, 2)
-        along_y, along_x = plane(s, (x + step) % 4, (y + step) % 4)
-        passed.append(send(along_y, [to_y[ahead]]) + send(along_x, [to_x[ahead]]))
-
+            send(along_y, to_y) + send(along_x, to_x)
+        )
     view = queries.reshape(16, 512, 128)
 
     def add_product(slab, first):
-        rows = jnp.concatenate([view[slab], view[slab + 1]], axis=1)
-        column = pl.ds(pl.multiple_of(slab * 128, 256), 256)
+        rows = jnp.concatenate([view[slab + j] for j in range(SPAN)], axis=1)
+        column = pl.ds(pl.multiple_of(slab * 128, 256), SPAN * 128)
 
         def tile(n, _):
             part_rows = pl.ds(pl.multiple_of(n * 256, 256), 256)
@@ -236,12 +230,14 @@
     load_store.wait()
     swaps = []
     for s in range(CHUNKS):
-        arrive(passed[s])
+        arrive(planes[s])
         swaps.append(send(queries.at[pl.ds(base + 2 * s, 2)], [partner]))
-        add_product(base + 2 * s, s == 0)
+        if (2 * s + 2) % SPAN == 0:
+            add_product(base + 2 * s + 2 - SPAN, 2 * s + 2 == SPAN)
     for s in range(CHUNKS):
         arrive(swaps[s])
-        add_product(other + 2 * s, False)
+        if (2 * s + 2) % SPAN == 0:
+            add_product(other + 2 * s + 2 - SPAN, False)
     for one in used:
         one.wait_send()
 
@@ -260,7 +256,7 @@
     kern = pl.pallas_call(
         influence_kernel,
         out_shape=jax.ShapeDtypeStruct((512, grad_store.shape[0]), jnp.float32),
-        in_specs=[pl.BlockSpec(memory_space=pl.ANY)] * len(operands),
+        in_specs=[pl.BlockSpec(memory_space=pltpu.HBM)] * len(operands),
         out_specs=pl.BlockSpec(memory_space=pltpu.VMEM),
         scratch_shapes=[
             *[pltpu.VMEM(one.shape, one.dtype) for one in operands],
@@ -275,10 +271,10 @@
             pltpu.SemaphoreType.DMA((COPIES,)),
         ],
         compiler_params=pltpu.CompilerParams(
-            collective_id=0, has_side_effects=True, vmem_limit_bytes=60 * 1024 * 1024
+            collective_id=0, has_side_effects=True, vmem_limit_bytes=32 * 1024 * 1024
         ),
     )
-    return kern(*operands)
+    return kern(*[pltpu.with_memory_space_constraint(one, pltpu.HBM) for one in operands])
 
 
 def solution(mesh):

time: 53.5 us -> 42.9 us (0.80)
  the two profiles are of different devices: /device:TPU:2 before, /device:TPU:1 now
where the time goes in v4:
time: 42.9 us; the launch traced here: 42.8 us
  Pallas kernels  41.1 us (96%)
  local copies, waits for them, and re-layouts  1.67 us (4%)
    pallas_call x1, Pallas kernels, on_device(): kern(*[pltpu.with_memory_space_constraint(one, pltpu.HBM) for one in oper...  41.1 us
    unnamed x1, local copies, waits for them, and re-layouts  1.67 us

profile of v4, /device:TPU:1, one launch (start us, length us, event | category | flops | bytes accessed | tf_op | source)
XLA Modules:
  0.0 42.8 jit_solution(9503141208129466263)
XLA Ops:
  0.0 41.1 %shard_map.73 = f32[512,1536]{1,0:T(8,128)S(1)} custom-call(bf16[1024,512]{1,0:T(8,128)(2,1)} %act_hbm.1, bf16[1024,512]{1,0:T(8,128)(2,1)} %grd_hbm.1, bf16[32,512]{1,0:T(8,128)(2,1)} %bitcast.3, bf16[64,512]{1,0:T(8,128)(2,1)} %bitcast.2, f32[32,32]{1,0:T(8,128)} %in_inv_hbm.1, f32[64,64]{1,0:T(8,128)} %out_inv_hbm.1, bf16[1536,2048]{1,0:T(8,128)(2,1)} %store_hbm.1), custom_call_target="tpu_custom_call" | custom-call | tf_op jit(solution)/shard_map/pallas_call | solution.py:277
  41.1 1.7 %copy.9 = f32[512,1536]{1,0:T(8,128)} copy(f32[512,1536]{1,0:T(8,128)S(1)} %shard_map.73) | data formatting | bytes 6291456

commit v5 on v4

--- a/solution.py
+++ b/solution.py
@@ -8,7 +8,7 @@
 from jax.sharding import PartitionSpec as P
 
 SEQ = 32
-SPAN = 8
+SPAN = 4
 MESH = pl.DeviceIdType.MESH
 NT = (((1,), (1,)), ((), ()))
 highest = lax.Precision.HIGHEST
@@ -81,7 +81,7 @@
     act_hbm, grd_hbm, win_hbm, wout_hbm, in_inv_hbm, out_inv_hbm, store_hbm,
     out_ref,
     act_ref, grd_ref, win_ref, wout_ref, in_inv_ref, out_inv_ref, store,
-    part, from_core, half, from_group, mine, queries,
+    part, from_core, half, from_group, mine, queries, level,
     load_sem, send_sem, recv_sem,
 ):
     loads = [
@@ -180,38 +180,50 @@
         for one in sent:
             one.wait_recv()
 
-    def line(s, x_, y_):
-        return (
-            queries.at[base + 2 * s, :, x_ % 2, y, x_ // 2],
-            queries.at[base + 2 * s + 1, :, xl, y_, xh],
+    left_already = set()
+
+    def leave(sent):
+        for one in sent:
+            one.wait_send()
+        left_already.update(id(one) for one in sent)
+
+    def split(h):
+        return pl.ds(base + 4 * h, 2), pl.ds(base + 4 * h + 2, 2)
+
+    def start_columns(h):
+        return send(queries.at[pl.ds(base + 4 * h, 4), z, xl, y, xh], to_z)
+
+    def start_lines(h):
+        first, second = split(h)
+        return send(queries.at[first, :, xl, y, xh], to_x) + send(
+            queries.at[second, :, xl, y, xh], to_y
         )
 
-    def plane(s, x_, y_):
-        return (
-            queries.at[base + 2 * s, :, :, y_],
-            queries.at[base + 2 * s + 1, :, x_ % 2, :, x_ // 2],
+    def start_planes(h):
+        first, second = split(h)
+        return send(queries.at[first, :, :, y], to_y) + send(
+            queries.at[second, :, xl, :, xh], to_x
         )
 
-    CHUNKS = 4
-    columns = [send(queries.at[pl.ds(base, 2), z, xl, y, xh], to_z)]
-    columns.append(send(queries.at[pl.ds(base + 2, 6), z, xl, y, xh], to_z))
-    lines = []
-    for s in range(CHUNKS):
-        if s < 2:
-            arrive(columns[s])
-        along_x, along_y = line(s, x, y)
-        lines.append(send(along_x, to_x) + send(along_y, to_y))
-    planes = []
-    for s in range(CHUNKS):
-        arrive(lines[s])
-        along_y, along_x = plane(s, x, y)
-        planes.append(
-            send(along_y, to_y) + send(along_x, to_x)
-        )
     view = queries.reshape(16, 512, 128)
 
-    def add_product(slab, first):
-        rows = jnp.concatenate([view[slab + j] for j in range(SPAN)], axis=1)
+    def start_swap(h):
+        span = pl.ds(base + 4 * h, 4)
+        one = copy(view.at[span], level.at[span], partner)
+        one.start()
+        return [one]
+
+    columns = [start_columns(0), start_columns(1)]
+    arrive(columns[0])
+    lines = [start_lines(0)]
+    arrive(columns[1])
+    lines.append(start_lines(1))
+    arrive(lines[0])
+    planes = [start_planes(0)]
+    arrive(lines[1])
+
+    def add_product(source, slab, first):
+        rows = jnp.concatenate([source[slab + j] for j in range(SPAN)], axis=1)
         column = pl.ds(pl.multiple_of(slab * 128, 256), SPAN * 128)
 
         def tile(n, _):
@@ -225,24 +237,26 @@
                 out_ref[:, part_rows] += term
             return 0
 
-        lax.fori_loop(0, store.shape[0] // 256, tile, 0)
+        lax.fori_loop(0, store.shape[0] // 256, tile, 0, unroll=6)
 
     load_store.wait()
-    swaps = []
-    for s in range(CHUNKS):
-        arrive(planes[s])
-        swaps.append(send(queries.at[pl.ds(base + 2 * s, 2)], [partner]))
-        if (2 * s + 2) % SPAN == 0:
-            add_product(base + 2 * s + 2 - SPAN, 2 * s + 2 == SPAN)
-    for s in range(CHUNKS):
-        arrive(swaps[s])
-        if (2 * s + 2) % SPAN == 0:
-            add_product(other + 2 * s + 2 - SPAN, False)
+    planes.append(start_planes(1))
+    arrive(planes[0])
+    swaps = [start_swap(0)]
+    add_product(view, base, True)
+    arrive(swaps[0])
+    add_product(level, other, False)
+    arrive(planes[1])
+    swaps.append(start_swap(1))
+    add_product(view, base + 4, False)
+    arrive(swaps[1])
+    add_product(level, other + 4, False)
     for one in used:
-        one.wait_send()
-
-
-COPIES = 1 + 7 + 1 + 2 * 7 + 4 * (6 + 4 + 2 + 1)
+        if id(one) not in left_already:
+            one.wait_send()
+
+
+COPIES = 1 + 7 + 1 + 2 * (7 + 6 + 6 + 1)
 
 
 def on_device(
@@ -266,6 +280,7 @@
             pltpu.VMEM((7, 48, 128), jnp.float32),
             pltpu.VMEM((16, 2, 128), jnp.bfloat16),
             pltpu.VMEM((16, 8, 2, 4, 2, 2, 2, 128), jnp.bfloat16),
+            pltpu.VMEM((16, 512, 128), jnp.bfloat16),
             pltpu.SemaphoreType.DMA((len(operands),)),
             pltpu.SemaphoreType.DMA((COPIES,)),
             pltpu.SemaphoreType.DMA((COPIES,)),

time: 42.9 us -> 40.8 us (0.951)
  Pallas kernels: 41.1 us -> 39.1 us
    pallas_call x1, Pallas kernels: 41.1 us -> 39.1 us  [on_device(): kern(*[pltpu.with_memory_space_constraint(one, pltpu.HBM) for one in oper...]
where the time goes in v5:
time: 40.8 us; the launch traced here: 40.7 us
  Pallas kernels  39.1 us (96%)
  local copies, waits for them, and re-layouts  1.67 us (4%)
    pallas_call x1, Pallas kernels, on_device(): kern(*[pltpu.with_memory_space_constraint(one, pltpu.HBM) for one in oper...  39.1 us
    unnamed x1, local copies, waits for them, and re-layouts  1.67 us

profile of v5, /device:TPU:1, one launch (start us, length us, event | category | flops | bytes accessed | tf_op | source)
XLA Modules:
  0.0 40.7 jit_solution(2171499773948467429)
XLA Ops:
  0.0 39.1 %shard_map.73 = f32[512,1536]{1,0:T(8,128)S(1)} custom-call(bf16[1024,512]{1,0:T(8,128)(2,1)} %act_hbm.1, bf16[1024,512]{1,0:T(8,128)(2,1)} %grd_hbm.1, bf16[32,512]{1,0:T(8,128)(2,1)} %bitcast.3, bf16[64,512]{1,0:T(8,128)(2,1)} %bitcast.2, f32[32,32]{1,0:T(8,128)} %in_inv_hbm.1, f32[64,64]{1,0:T(8,128)} %out_inv_hbm.1, bf16[1536,2048]{1,0:T(8,128)(2,1)} %store_hbm.1), custom_call_target="tpu_custom_call" | custom-call | tf_op jit(solution)/shard_map/pallas_call | solution.py:292
  39.1 1.7 %copy.9 = f32[512,1536]{1,0:T(8,128)} copy(f32[512,1536]{1,0:T(8,128)S(1)} %shard_map.73) | data formatting | bytes 6291456

commit v6 on v5

--- a/solution.py
+++ b/solution.py
@@ -8,7 +8,7 @@
 from jax.sharding import PartitionSpec as P
 
 SEQ = 32
-SPAN = 4
+SPAN = 8
 MESH = pl.DeviceIdType.MESH
 NT = (((1,), (1,)), ((), ()))
 highest = lax.Precision.HIGHEST
@@ -106,7 +106,7 @@
     def device(y_, x_, z_, c_):
         return (y_, 2 * (x_ // 2) + c_, 2 * z_ + x_ % 2)
 
-    group = [(dy, dx) for dy in range(ny) for dx in (0, 2) if (dy, dx) != (0, 0)]
+    group = [(2, 2), (1, 2), (3, 2), (2, 0), (0, 2), (1, 0), (3, 0)]
     partner = device(y, x, z, oc)
     to_group = [device((y + dy) % ny, (x + dx) % 4, z, c) for dy, dx in group]
     to_z = [device(y, x, (z + d) % nz, c) for d in range(1, nz)]
@@ -180,47 +180,52 @@
         for one in sent:
             one.wait_recv()
 
-    left_already = set()
-
-    def leave(sent):
-        for one in sent:
-            one.wait_send()
-        left_already.update(id(one) for one in sent)
-
-    def split(h):
-        return pl.ds(base + 4 * h, 2), pl.ds(base + 4 * h + 2, 2)
-
-    def start_columns(h):
-        return send(queries.at[pl.ds(base + 4 * h, 4), z, xl, y, xh], to_z)
-
-    def start_lines(h):
-        first, second = split(h)
-        return send(queries.at[first, :, xl, y, xh], to_x) + send(
-            queries.at[second, :, xl, y, xh], to_y
+    view = queries.reshape(16, 512, 128)
+    first, second = pl.ds(base, 4), pl.ds(base + 4, 4)
+    far_x, far_y = [to_x[1], to_x[0], to_x[2]], [to_y[1], to_y[0], to_y[2]]
+
+    def start_lines(z_):
+        return send(queries.at[first, z_, xl, y, xh], far_x) + send(
+            queries.at[second, z_, xl, y, xh], far_y
         )
 
-    def start_planes(h):
-        first, second = split(h)
-        return send(queries.at[first, :, :, y], to_y) + send(
-            queries.at[second, :, xl, :, xh], to_x
+    def start_planes(z_):
+        return send(queries.at[first, z_, :, y], far_y) + send(
+            queries.at[second, z_, xl, :, xh], far_x
         )
 
-    view = queries.reshape(16, 512, 128)
-
-    def start_swap(h):
-        span = pl.ds(base + 4 * h, 4)
-        one = copy(view.at[span], level.at[span], partner)
+    def start_swap(z_):
+        rows = pl.ds(pl.multiple_of(64 * z_, 64), 64)
+        one = copy(view.at[own, rows], level.at[own, rows], partner)
         one.start()
         return [one]
 
-    columns = [start_columns(0), start_columns(1)]
-    arrive(columns[0])
-    lines = [start_lines(0)]
-    arrive(columns[1])
-    lines.append(start_lines(1))
-    arrive(lines[0])
-    planes = [start_planes(0)]
-    arrive(lines[1])
+    def block(d):
+        return (z + nz - d) % nz
+
+    columns, lines, planes, swaps = {}, {}, {}, {}
+    for d in (4, 3, 5, 2, 6, 1, 7):
+        columns[d] = send(queries.at[own, z, xl, y, xh], [to_z[d - 1]])
+    lines[0] = start_lines(z)
+
+    def next_line(d):
+        arrive(columns[d])
+        lines[d] = start_lines(block(d))
+
+    def next_plane(d):
+        arrive(lines[d])
+        planes[d] = start_planes(block(d))
+
+    for d in (1, 7, 2, 6):
+        next_line(d)
+    next_plane(0)
+    for d in (3, 5, 4):
+        next_line(d)
+    for d in (1, 7, 2, 6, 3, 5, 4):
+        next_plane(d)
+    for d in (0, 1, 7, 2, 6, 3, 5, 4):
+        arrive(planes[d])
+        swaps[d] = start_swap(block(d))
 
     def add_product(source, slab, first):
         rows = jnp.concatenate([source[slab + j] for j in range(SPAN)], axis=1)
@@ -240,23 +245,15 @@
         lax.fori_loop(0, store.shape[0] // 256, tile, 0, unroll=6)
 
     load_store.wait()
-    planes.append(start_planes(1))
-    arrive(planes[0])
-    swaps = [start_swap(0)]
     add_product(view, base, True)
-    arrive(swaps[0])
+    for d in range(nz):
+        arrive(swaps[d])
     add_product(level, other, False)
-    arrive(planes[1])
-    swaps.append(start_swap(1))
-    add_product(view, base + 4, False)
-    arrive(swaps[1])
-    add_product(level, other + 4, False)
     for one in used:
-        if id(one) not in left_already:
-            one.wait_send()
-
-
-COPIES = 1 + 7 + 1 + 2 * (7 + 6 + 6 + 1)
+        one.wait_send()
+
+
+COPIES = 1 + 7 + 1 + 7 + 8 * (6 + 6 + 1)
 
 
 def on_device(

time: 40.8 us -> 39.1 us (0.958)
  Pallas kernels: 39.1 us -> 37.3 us
    pallas_call x1, Pallas kernels: 39.1 us -> 37.3 us  [on_device(): kern(*[pltpu.with_memory_space_constraint(one, pltpu.HBM) for one in oper...]
where the time goes in v6:
time: 39.1 us; the launch traced here: 39 us
  Pallas kernels  37.3 us (95%)
  local copies, waits for them, and re-layouts  1.67 us (4%)
    pallas_call x1, Pallas kernels, on_device(): kern(*[pltpu.with_memory_space_constraint(one, pltpu.HBM) for one in oper...  37.3 us
    unnamed x1, local copies, waits for them, and re-layouts  1.67 us

profile of v6, /device:TPU:1, one launch (start us, length us, event | category | flops | bytes accessed | tf_op | source)
XLA Modules:
  0.0 39.0 jit_solution(9562476860243026710)
XLA Ops:
  0.0 37.3 %shard_map.73 = f32[512,1536]{1,0:T(8,128)S(1)} custom-call(bf16[1024,512]{1,0:T(8,128)(2,1)} %act_hbm.1, bf16[1024,512]{1,0:T(8,128)(2,1)} %grd_hbm.1, bf16[32,512]{1,0:T(8,128)(2,1)} %bitcast.3, bf16[64,512]{1,0:T(8,128)(2,1)} %bitcast.2, f32[32,32]{1,0:T(8,128)} %in_inv_hbm.1, f32[64,64]{1,0:T(8,128)} %out_inv_hbm.1, bf16[1536,2048]{1,0:T(8,128)(2,1)} %store_hbm.1), custom_call_target="tpu_custom_call" | custom-call | tf_op jit(solution)/shard_map/pallas_call | solution.py:289
  37.3 1.7 %copy.9 = f32[512,1536]{1,0:T(8,128)} copy(f32[512,1536]{1,0:T(8,128)S(1)} %shard_map.73) | data formatting | bytes 6291456

commit v7 on v6

--- a/solution.py
+++ b/solution.py
@@ -9,6 +9,8 @@
 
 SEQ = 32
 SPAN = 8
+REL = (0, 1, 7, 2, 6, 3, 5, 4)
+RUNS = ((0, 1), (1, 2), (3, 2), (5, 3))
 MESH = pl.DeviceIdType.MESH
 NT = (((1,), (1,)), ((), ()))
 highest = lax.Precision.HIGHEST
@@ -165,9 +167,9 @@
 
     base, other = 8 * c, 8 * oc
     own = pl.ds(base, 8)
-    swap = copy(mine.at[pl.ds(other, 8)], queries.at[pl.ds(other, 8), z, xl, y, xh, c], partner)
+    swap = copy(mine.at[pl.ds(other, 8)], queries.at[pl.ds(other, 8), 0, xl, y, xh, c], partner)
     swap.start()
-    queries[own, z, xl, y, xh, c] = mine[own]
+    queries[own, 0, xl, y, xh, c] = mine[own]
     swap.wait_recv()
 
     def send(view, peers):
@@ -184,76 +186,84 @@
     first, second = pl.ds(base, 4), pl.ds(base + 4, 4)
     far_x, far_y = [to_x[1], to_x[0], to_x[2]], [to_y[1], to_y[0], to_y[2]]
 
-    def start_lines(z_):
-        return send(queries.at[first, z_, xl, y, xh], far_x) + send(
-            queries.at[second, z_, xl, y, xh], far_y
+    def start_lines(run):
+        at = pl.ds(*run)
+        return send(queries.at[first, at, xl, y, xh], far_x) + send(
+            queries.at[second, at, xl, y, xh], far_y
         )
 
-    def start_planes(z_):
-        return send(queries.at[first, z_, :, y], far_y) + send(
-            queries.at[second, z_, xl, :, xh], far_x
+    def start_planes(run):
+        at = pl.ds(*run)
+        return send(queries.at[first, at, :, y], far_y) + send(
+            queries.at[second, at, xl, :, xh], far_x
         )
 
-    def start_swap(z_):
-        rows = pl.ds(pl.multiple_of(64 * z_, 64), 64)
+    def start_swap(run):
+        rows = pl.ds(64 * run[0], 64 * run[1])
         one = copy(view.at[own, rows], level.at[own, rows], partner)
         one.start()
         return [one]
 
-    def block(d):
-        return (z + nz - d) % nz
-
-    columns, lines, planes, swaps = {}, {}, {}, {}
-    for d in (4, 3, 5, 2, 6, 1, 7):
-        columns[d] = send(queries.at[own, z, xl, y, xh], [to_z[d - 1]])
-    lines[0] = start_lines(z)
-
-    def next_line(d):
-        arrive(columns[d])
-        lines[d] = start_lines(block(d))
-
-    def next_plane(d):
-        arrive(lines[d])
-        planes[d] = start_planes(block(d))
-
-    for d in (1, 7, 2, 6):
-        next_line(d)
-    next_plane(0)
-    for d in (3, 5, 4):
-        next_line(d)
-    for d in (1, 7, 2, 6, 3, 5, 4):
-        next_plane(d)
-    for d in (0, 1, 7, 2, 6, 3, 5, 4):
-        arrive(planes[d])
-        swaps[d] = start_swap(block(d))
+    columns, lines, planes, swaps = {}, [], [], []
+    for r in (4, 3, 5, 2, 6, 1, 7):
+        columns[r] = copy(
+            queries.at[own, 0, xl, y, xh],
+            queries.at[own, REL.index(r), xl, y, xh],
+            to_z[nz - r - 1],
+        )
+        columns[r].start()
+    lines.append(start_lines(RUNS[0]))
+
+    def next_line():
+        run = RUNS[len(lines)]
+        arrive([columns[r] for r in REL[run[0] : run[0] + run[1]]])
+        lines.append(start_lines(run))
+
+    def next_plane():
+        arrive(lines[len(planes)])
+        planes.append(start_planes(RUNS[len(planes)]))
+
+    next_line()
+    next_line()
+    next_plane()
+    next_line()
+    next_plane()
+    next_plane()
+    next_plane()
+    for n, run in enumerate(RUNS):
+        arrive(planes[n])
+        swaps.append(start_swap(run))
 
     def add_product(source, slab, first):
         rows = jnp.concatenate([source[slab + j] for j in range(SPAN)], axis=1)
         column = pl.ds(pl.multiple_of(slab * 128, 256), SPAN * 128)
 
-        def tile(n, _):
-            part_rows = pl.ds(pl.multiple_of(n * 256, 256), 256)
+        def tile(step, _):
+            part_rows = pl.ds(pl.multiple_of(step * 256, 256), 256)
             term = lax.dot_general(
                 rows, store[part_rows, column], NT, preferred_element_type=jnp.float32
             )
-            if first:
-                out_ref[:, part_rows] = term
-            else:
-                out_ref[:, part_rows] += term
+            for n, r in enumerate(REL):
+                to = pl.ds(pl.multiple_of(64 * lax.rem(z + r, nz), 64), 64)
+                block = term[64 * n : 64 * n + 64]
+                if first:
+                    out_ref[to, part_rows] = block
+                else:
+                    out_ref[to, part_rows] += block
             return 0
 
         lax.fori_loop(0, store.shape[0] // 256, tile, 0, unroll=6)
 
     load_store.wait()
     add_product(view, base, True)
-    for d in range(nz):
-        arrive(swaps[d])
+    for one in swaps:
+        arrive(one)
     add_product(level, other, False)
     for one in used:
         one.wait_send()
 
 
-COPIES = 1 + 7 + 1 + 7 + 8 * (6 + 6 + 1)
+COPIES = 1 + 7 + 1 + 7 + len(RUNS) * (6 + 6 + 1)
 
 
 def on_device(

time: 39.1 us -> 38.5 us (0.985)
  Pallas kernels: 37.3 us -> 36.7 us
    pallas_call x1, Pallas kernels: 37.3 us -> 36.7 us  [on_device(): kern(*[pltpu.with_memory_space_constraint(one, pltpu.HBM) for one in oper...]
where the time goes in v7:
time: 38.5 us; the launch traced here: 38.4 us
  Pallas kernels  36.7 us (95%)
  local copies, waits for them, and re-layouts  1.67 us (4%)
    pallas_call x1, Pallas kernels, on_device(): kern(*[pltpu.with_memory_space_constraint(one, pltpu.HBM) for one in oper...  36.7 us
    unnamed x1, local copies, waits for them, and re-layouts  1.67 us

profile of v7, /device:TPU:1, one launch (start us, length us, event | category | flops | bytes accessed | tf_op | source)
XLA Modules:
  0.0 38.4 jit_solution(7412690260703006464)
XLA Ops:
  0.0 36.7 %shard_map.73 = f32[512,1536]{1,0:T(8,128)S(1)} custom-call(bf16[1024,512]{1,0:T(8,128)(2,1)} %act_hbm.1, bf16[1024,512]{1,0:T(8,128)(2,1)} %grd_hbm.1, bf16[32,512]{1,0:T(8,128)(2,1)} %bitcast.3, bf16[64,512]{1,0:T(8,128)(2,1)} %bitcast.2, f32[32,32]{1,0:T(8,128)} %in_inv_hbm.1, f32[64,64]{1,0:T(8,128)} %out_inv_hbm.1, bf16[1536,2048]{1,0:T(8,128)(2,1)} %store_hbm.1), custom_call_target="tpu_custom_call" | custom-call | tf_op jit(solution)/shard_map/pallas_call | solution.py:299
  36.8 1.7 %copy.9 = f32[512,1536]{1,0:T(8,128)} copy(f32[512,1536]{1,0:T(8,128)S(1)} %shard_map.73) | data formatting | bytes 6291456

commit v8 on v7

--- a/solution.py
+++ b/solution.py
@@ -83,7 +83,7 @@
     act_hbm, grd_hbm, win_hbm, wout_hbm, in_inv_hbm, out_inv_hbm, store_hbm,
     out_ref,
     act_ref, grd_ref, win_ref, wout_ref, in_inv_ref, out_inv_ref, store,
-    part, from_core, half, from_group, mine, queries, level,
+    part, from_core, half, from_group, mine, theirs, queries, level,
     load_sem, send_sem, recv_sem,
 ):
     loads = [
@@ -167,10 +167,14 @@
 
     base, other = 8 * c, 8 * oc
     own = pl.ds(base, 8)
-    swap = copy(mine.at[pl.ds(other, 8)], queries.at[pl.ds(other, 8), 0, xl, y, xh, c], partner)
+    swap = copy(mine.at[pl.ds(other, 8)], theirs, partner)
     swap.start()
-    queries[own, 0, xl, y, xh, c] = mine[own]
     swap.wait_recv()
+    for j in range(8):
+        one, two = mine[base + j], theirs[j]
+        queries[base + j, 0, xl, y, xh] = jnp.where(
+            c == 0, jnp.concatenate([one, two], axis=0), jnp.concatenate([two, one], axis=0)
+        )
 
     def send(view, peers):
         sent = [copy(view, view, peer) for peer in peers]
@@ -286,7 +290,8 @@
             pltpu.VMEM((pairs // 2, 48, 128), jnp.float32),
             pltpu.VMEM((7, 48, 128), jnp.float32),
             pltpu.VMEM((16, 2, 128), jnp.bfloat16),
-            pltpu.VMEM((16, 8, 2, 4, 2, 2, 2, 128), jnp.bfloat16),
+            pltpu.VMEM((8, 2, 128), jnp.bfloat16),
+            pltpu.VMEM((16, 8, 2, 4, 2, 4, 128), jnp.bfloat16),
             pltpu.VMEM((16, 512, 128), jnp.bfloat16),
             pltpu.SemaphoreType.DMA((len(operands),)),
             pltpu.SemaphoreType.DMA((COPIES,)),

time: 38.5 us -> 38.6 us (level)
  no operation moved by 1% of the time
where the time goes in v8:
time: 38.6 us; the launch traced here: 38.5 us
  Pallas kernels  36.8 us (95%)
  local copies, waits for them, and re-layouts  1.67 us (4%)
    pallas_call x1, Pallas kernels, on_device(): kern(*[pltpu.with_memory_space_constraint(one, pltpu.HBM) for one in oper...  36.8 us
    unnamed x1, local copies, waits for them, and re-layouts  1.67 us

profile of v8, /device:TPU:1, one launch (start us, length us, event | category | flops | bytes accessed | tf_op | source)
XLA Modules:
  0.0 38.5 jit_solution(3981717988481998623)
XLA Ops:
  0.0 36.8 %shard_map.73 = f32[512,1536]{1,0:T(8,128)S(1)} custom-call(bf16[1024,512]{1,0:T(8,128)(2,1)} %act_hbm.1, bf16[1024,512]{1,0:T(8,128)(2,1)} %grd_hbm.1, bf16[32,512]{1,0:T(8,128)(2,1)} %bitcast.3, bf16[64,512]{1,0:T(8,128)(2,1)} %bitcast.2, f32[32,32]{1,0:T(8,128)} %in_inv_hbm.1, f32[64,64]{1,0:T(8,128)} %out_inv_hbm.1, bf16[1536,2048]{1,0:T(8,128)(2,1)} %store_hbm.1), custom_call_target="tpu_custom_call" | custom-call | tf_op jit(solution)/shard_map/pallas_call | solution.py:304
  36.8 1.7 %copy.9 = f32[512,1536]{1,0:T(8,128)} copy(f32[512,1536]{1,0:T(8,128)S(1)} %shard_map.73) | data formatting | bytes 6291456
